TPU v7x, 32 devices: a whole 2x2x4 slice. The times are simulated.
32 devices in a mesh: group: 2 (over y), row: 4 (over z), col: 2 (over x), sub: 2 (over core).
Axes of the slice: x: 2, y: 2, z: 4, core: 2. Of those that a mesh axis runs over, the one named last changes fastest.
Arguments:
- anomalies: bfloat16 [2048, 2048], P(('group', 'row', 'sub')), parts along dimension 0, may hold values from -6 to 6
- innovations: float32 [4096], P(('group', 'row', 'col', 'sub')), parts along dimension 0, may hold values from -12 to 12
- obs_error: float32 [4096], P(('group', 'row', 'col', 'sub')), parts along dimension 0, may hold values from 0.5 to 2
- track_pos: float32 [4096], P('group'), parts along dimension 0, may hold values from 0 to 1
- taper_class: int32 [8, 4], P('group'), parts along dimension 0, may hold values from 0 to 3, as said below
Outputs:
- solution: float32 [4096], P(('group', 'row', 'col', 'sub')), parts along dimension 0
- residual: float32 [4096], P(('group', 'row', 'col', 'sub')), parts along dimension 0
There are 2 independent parts, one for each index of `group`. A program takes and returns all parts, laid end to end along the dimension named above; each array names one. Nothing has to cross between parts.
Inputs may be any that keep to these rules, and one draw needn't show every extreme that they name: `taper_class`: tiles are spatial blocks of the region, laid along the plume in an order given by a permutation pos of the 4 tiles; entry (a, b) is the distance |pos[a] - pos[b]| in tiles.
All inputs are finite; a program needn't handle non-finite values.
Results may differ from a plain program's by a relative error of at most 0.0003.
Values may be sent and summed in bfloat16 or wider, within the bound.
No kernel may reach another device: no remote copies, remote signals or barrier semaphores. Data moves between devices by JAX's collectives and lax.ppermute only.
A program may use at most 64 MiB of HBM per device.

v0:
```python
import jax
import jax.numpy as jnp
from jax import lax
from jax.sharding import PartitionSpec as P

ITERS = 2
track_width = 0.0001


def squares(residual):
    return lax.psum(jnp.sum(residual * residual), ("row", "col", "sub"))


def per_device(anomalies, innovations, obs_error, track_pos, taper_class):
    row_count = lax.axis_size("row")
    col_count = lax.axis_size("col")
    sub_count = lax.axis_size("sub")
    row_index = lax.axis_index("row")
    col_index = lax.axis_index("col")
    local_members, total_obs = anomalies.shape
    block_len = total_obs // row_count
    quarter_len = block_len // col_count
    member_total = local_members * row_count * sub_count
    inverse_members = 1.0 / (member_total - 1)
    reach_tiles = max(2, row_count // 4)
    class_row = lax.dynamic_index_in_dim(taper_class, row_index, 0, keepdims=False)
    tile_weight = jnp.maximum(0.0, 1.0 - class_row.astype(jnp.float32) / reach_tiles)
    row_pos = lax.dynamic_slice_in_dim(track_pos, row_index * block_len, block_len, 0)
    col_pos = lax.dynamic_index_in_dim(
        track_pos.reshape(row_count, col_count, quarter_len), col_index, 1, keepdims=False
    )
    own_block = lax.all_to_all(anomalies, "row", split_axis=1, concat_axis=0, tiled=True)
    own_quarter = lax.dynamic_slice_in_dim(own_block, col_index * quarter_len, quarter_len, 1)

    def one_tile(piece, block_index, keep_factor):
        product = jnp.einsum("mi,mq->iq", own_block, piece, preferred_element_type=jnp.float32)
        column_pos = lax.dynamic_index_in_dim(col_pos, block_index, 0, keepdims=False)
        weight_here = lax.dynamic_index_in_dim(tile_weight, block_index, 0, keepdims=False)
        distance = row_pos[:, None] - column_pos[None, :]
        taper = weight_here * keep_factor * jnp.exp(-(distance * distance) / track_width)
        return product * (taper * inverse_members)

    def one_entry(entry):
        return one_tile(entry[0], entry[1], 1.0)

    piece = lax.all_gather(own_quarter[None], "row", axis=0, tiled=True)
    indices = jnp.arange(piece.shape[0], dtype=jnp.int32)
    tiles = lax.map(one_entry, (piece, indices))
    solution = jnp.zeros_like(innovations)
    residual = innovations
    direction_vec = innovations
    norm_now = squares(residual)
    for turn_index in range(ITERS):
        column_vec = lax.all_gather(direction_vec, ("row", "sub"), axis=0, tiled=True).reshape(
            row_count, quarter_len
        )
        direct = jnp.einsum("jiq,jq->i", tiles, column_vec, precision=lax.Precision.HIGHEST)
        extra = obs_error * direction_vec
        own_part = lax.psum_scatter(direct, ("col", "sub"), scatter_dimension=0, tiled=True)
        image = own_part + extra
        alpha = norm_now / lax.psum(jnp.sum(direction_vec * image), ("row", "col", "sub"))
        solution = solution + alpha * direction_vec
        residual = residual - alpha * image
        if turn_index + 1 < ITERS:
            norm_next = squares(residual)
            direction_vec = residual + norm_next / norm_now * direction_vec
            norm_now = norm_next
    return (solution, residual)


def solution(mesh):
    in_specs = (
        P(("group", "row", "sub"), None),
        P(("group", "row", "col", "sub")),
        P(("group", "row", "col", "sub")),
        P("group"),
        P("group", None),
    )
    out_specs = (P(("group", "row", "col", "sub")), P(("group", "row", "col", "sub")))
    return jax.shard_map(
        per_device, mesh=mesh, in_specs=in_specs, out_specs=out_specs, check_vma=False
    )
```

profile of v0, /device:TPU:0, one launch (start us, length us, event | category | flops | bytes accessed | tf_op | source)
XLA Modules:
  0.0 207.6 jit_solution(16276653144272945120)
XLA Ops:
  7.2 0.0 copy-start.3
  7.2 0.0 copy-start
  7.2 0.0 copy-start.1
  7.2 1.9 copy.16
  9.1 6.3 %all-to-all-start = ((bf16[128,4,512]{2,0,1:T(8,128)(2,1)}), bf16[128,4,512]{2,0,1:T(8,128)(2,1)S(1)}, u32[]{:S(2)}, u32[]{:S(2)}) async-start(bf16[128,4,512]{2,0,1:T(8,128)(2,1)} %bitcast.41), calls=%async_computation | async-start | bytes 1048576 | tf_op jit(solution)/shard_map/all_to_all | solution.py:32
  15.4 0.0 all-gather.5.cloned.1.call-start
  15.4 14.5 %all-to-all-done = bf16[128,4,512]{2,0,1:T(8,128)(2,1)S(1)} async-done(((bf16[128,4,512]{2,0,1:T(8,128)(2,1)}), bf16[128,4,512]{2,0,1:T(8,128)(2,1)S(1)}, u32[]{:S(2)}, u32[]{:S(2)}) %all-to-all-start) | async-done | bytes 524320 | tf_op jit(solution)/shard_map/all_to_all | solution.py:32
  29.9 0.7 constant_dynamic-slice_fusion.3
  30.6 0.0 all-gather.5.cloned.1.call-update
  30.7 0.0 copy-done
  30.7 0.1 dynamic_slice.32
  30.8 0.0 copy-done.3
  30.8 0.6 dynamic-slice
  32.0 0.0 copy-done.1
  32.1 9.8 %all-gather.1 = f32[8,1,128]{2,1,0:T(1,128)S(1)} all-gather(f32[1,1,128]{2,1,0:T(1,128)S(1)} %bitcast.64), channel_id=1, replica_groups=mesh['group'=2,'row'=4,'col'=2,'sub'=2] {'row','sub'}, dimensions={0}, use_global_device_ids=true | all-gather | bytes 4608 | tf_op jit(solution)/shard_map/all_gather | solution.py:54
  41.8 0.7 maximum_bitcast_fusion
  42.5 15.3 %all-gather.5.cloned.1.call-done = bf16[2048,256]{1,0:T(8,128)(2,1)} async-done(((bf16[512,256]{1,0:T(8,128)(2,1)}), bf16[2048,256]{1,0:T(8,128)(2,1)}) %all-gather.5.cloned.1.call-update) | async-done | bytes 1048592 | tf_op jit(solution)/shard_map/all_gather | solution.py:46
  57.8 20.4 %while.10 = (s32[]{:T(128)}, f32[4,512,256]{1,2,0:T(8,128)S(1)}, bf16[4,512,256]{2,1,0:T(8,128)(2,1)}, bf16[512,512]{1,0:T(8,128)(2,1)S(1)}, s32[4]{0:T(128)S(1)...) while((s32[]{:T(128)}, f32[4,512,256]{1,2,0:T(8,128)S(1)}, ...), condition=%wide.region_3.4_spmd, body=%wide.region_2.3_spmd.sunk | while | flops 135135232 | bytes 1317547 | solution.py:48
  57.8 0.6 dynamic_slice.56
  60.4 0.6 dynamic_slice.57
  61.0 1.9 fusion.21
  62.9 0.6 dynamic_slice.56
  65.5 0.6 dynamic_slice.57
  66.1 1.9 fusion.21
  68.0 0.6 dynamic_slice.56
  70.6 0.6 dynamic_slice.57
  71.2 1.9 fusion.21
  73.1 0.6 dynamic_slice.56
  75.7 0.6 dynamic_slice.57
  76.3 1.9 fusion.21
  78.2 0.0 copy-start.2
  78.2 1.2 fusion.9
  79.4 6.4 %all-reduce = f32[512]{0:T(512)S(1)} all-reduce(f32[512]{0:T(512)S(1)} %bitcast.66), channel_id=3, replica_groups=mesh['group'=2,'row'=4,'col'=2,'sub'=2] {'col','sub'}, use_global_device_ids=true, to_apply=%region_4.5.clone | all-reduce | flops 512 | bytes 4096
  85.8 0.0 copy-done.2
  85.8 0.7 multiply_reduce_fusion.2
  86.5 31.6 %all-reduce.2 = (f32[]{:T(128)}, f32[]{:T(128)}) all-reduce(f32[]{:T(128)} %get-tuple-element.46, f32[]{:T(128)} %get-tuple-element.45), channel_id=1, replica_groups=mesh['group'=2,'row'=4,'col'=2,'sub'=2] {'row','col','sub'}, use_global_device_ids=true, to_apply=%region_1.2 | all-reduce | flops 2 | bytes 16 | tf_op jit(solution)/shard_map/psum | solution.py:11
  119.5 0.7 multiply_reduce_fusion.1
  120.1 30.1 %psum.30 = f32[]{:T(128)} all-reduce(f32[]{:T(128)} %get-tuple-element.65), channel_id=1, replica_groups=mesh['group'=2,'row'=4,'col'=2,'sub'=2] {'row','col','sub'}, use_global_device_ids=true, to_apply=%region_8.9 | all-reduce | flops 1 | bytes 8 | tf_op jit(solution)/shard_map/psum | solution.py:11
  151.6 8.4 %all-gather.2 = f32[8,1,128]{2,1,0:T(1,128)S(1)} all-gather(f32[1,1,128]{2,1,0:T(1,128)S(1)} %bitcast.67), channel_id=1, replica_groups=mesh['group'=2,'row'=4,'col'=2,'sub'=2] {'row','sub'}, dimensions={0}, use_global_device_ids=true | all-gather | bytes 4608 | tf_op jit(solution)/shard_map/all_gather | solution.py:54
  160.0 1.2 fusion.10
  161.2 5.9 %all-reduce.1 = f32[512]{0:T(512)S(1)} all-reduce(f32[512]{0:T(512)S(1)} %bitcast.65), channel_id=4, replica_groups=mesh['group'=2,'row'=4,'col'=2,'sub'=2] {'col','sub'}, use_global_device_ids=true, to_apply=%region_9.10.clone | all-reduce | flops 512 | bytes 4096
  167.1 0.7 multiply_reduce_fusion
  167.8 31.1 %psum.31 = f32[]{:T(128)} all-reduce(f32[]{:T(128)} %multiply_reduce_fusion), channel_id=1, replica_groups=mesh['group'=2,'row'=4,'col'=2,'sub'=2] {'row','col','sub'}, use_global_device_ids=true, to_apply=%region_11.12 | all-reduce | flops 1 | bytes 8 | tf_op jit(solution)/shard_map/psum | solution.py:61
  200.2 0.6 multiply_subtract_fusion
  (10 shorter events, 0.1 us)
Async XLA Ops:
  7.2 23.6 %copy-start.3 = (u32[32]{0:T(128)S(1)}, u32[32]{0:T(128)}, u32[]{:S(2)}) copy-start(u32[32]{0:T(128)} %constant.61) | copy-start | bytes 388
  7.2 23.5 %copy-start = (f32[2048]{0:T(1024)S(1)}, f32[2048]{0:T(1024)}, u32[]{:S(2)}) copy-start(f32[2048]{0:T(1024)} %param.10) | copy-start | bytes 24580
  7.2 24.9 %copy-start.1 = (f32[128]{0:T(128)S(1)}, f32[128]{0:T(128)}, u32[]{:S(2)}) copy-start(f32[128]{0:T(128)} %param.8) | copy-start | bytes 1540
  9.1 20.8 %all-to-all-start = ((bf16[128,4,512]{2,0,1:T(8,128)(2,1)}), bf16[128,4,512]{2,0,1:T(8,128)(2,1)S(1)}, u32[]{:S(2)}, u32[]{:S(2)}) async-start(bf16[128,4,512]{2,0,1:T(8,128)(2,1)} %bitcast.41), calls=%async_computation | async-start | bytes 1048576 | tf_op jit(solution)/shard_map/all_to_all | solution.py:32
  15.4 42.4 %all-gather.5.cloned.1.call-start = ((), (), s32[]{:S(2)}) async-start(), calls=%async_computation.1 | async-start | bytes 1310720 | tf_op jit(solution)/shard_map/all_gather | solution.py:46
  78.2 7.6 %copy-start.2 = (f32[128]{0:T(128)S(1)}, f32[128]{0:T(128)}, u32[]{:S(2)}) copy-start(f32[128]{0:T(128)} %param.9) | copy-start | bytes 1540
Sparse Core Ops, SparseCore 0:
  30.8 27.0 all-gather.4
where the time goes:
time: 208 us
  blocking collectives  123 us (59%)
  waiting for transfers between devices  29.8 us (14%)
  between operations  18.8 us (9%)
  matrix products  10.1 us (5%)
  local copies, waits for them, and re-layouts  8.07 us (4%)
  loops' own time  7.89 us (4%)
  starting transfers between devices  6.32 us (3%)
  other arithmetic  3.32 us (2%)
    psum x2, blocking collectives, squares(): return lax.psum(jnp.sum(residual * residual), ('row', 'col', 'sub'))  61.7 us
    psum x1, blocking collectives, per_device(): lax.psum(jnp.sum(direction_vec * image), ('row', 'col', 'sub'))  31.1 us
    all_gather x2, blocking collectives, per_device(): lax.all_gather(direction_vec, ('row', 'sub'), axis=0, tiled=True)  18.2 us
    all_gather x1, waiting for transfers between devices, per_device(): piece = lax.all_gather(own_quarter[None], 'row', axis=0, tiled=True)  15.3 us
    all_to_all x1, waiting for transfers between devices, per_device(): lax.all_to_all(anomalies, 'row', split_axis=1, concat_axis=0, tiled=True)  14.5 us
    unnamed x2, blocking collectives  12.3 us
    another operation x1, loops' own time, per_device(): tiles = lax.map(one_entry, (piece, indices))  7.89 us
    dot_general x4, matrix products, one_tile(): jnp.einsum('mi,mq->iq', own_block, piece, preferred_element_type=jnp.floa...  7.74 us
  transfers between devices with their start and end apart: 2, of which 2 were waited for; matrix products, arithmetic and copies ran while one was open for 1% of the time, Pallas kernels for 0%

commit v1 on v0

--- a/solution.py
+++ b/solution.py
@@ -1,3 +1,4 @@
+import functools
 import jax
 import jax.numpy as jnp
 from jax import lax
@@ -5,6 +6,34 @@
 
 ITERS = 2
 track_width = 0.0001
+
+
+def track_seats_all(q_in, comm_axis):
+    reached, value_now, opened = (
+        jax.lax.axis_size(comm_axis),
+        jax.lax.axis_index(comm_axis),
+        q_in.shape[0],
+    )
+    buffer = list(map(lambda it: (it, (it + 1) % reached), range(reached)))
+    inbox = list(map(lambda it: (it, (it - 1) % reached), range(reached)))
+    m_next = jnp.zeros((*q_in.shape[:0], reached * opened, *q_in.shape[1:]), q_in.dtype)
+    m_next = lax.dynamic_update_slice_in_dim(m_next, q_in, value_now * opened, axis=0)
+    tile_out = piece_next = q_in
+    w_next = reached // 2
+    for dev_i in [*range(1, w_next + 1)]:
+        tile_out = jax.lax.ppermute(tile_out, comm_axis, buffer)
+        m_next = lax.dynamic_update_slice_in_dim(
+            m_next, tile_out, (value_now - dev_i) % reached * opened, axis=0
+        )
+        if dev_i < reached - w_next:
+            piece_next = jax.lax.ppermute(piece_next, comm_axis, inbox)
+            m_next = lax.dynamic_update_slice_in_dim(
+                m_next, piece_next, (value_now + dev_i) % reached * opened, axis=0
+            )
+    return m_next
+
+
+store_tasks = functools.partial(track_seats_all, comm_axis=("row", "sub"))
 
 
 def squares(residual):
@@ -51,9 +80,7 @@
     direction_vec = innovations
     norm_now = squares(residual)
     for turn_index in range(ITERS):
-        column_vec = lax.all_gather(direction_vec, ("row", "sub"), axis=0, tiled=True).reshape(
-            row_count, quarter_len
-        )
+        column_vec = store_tasks(direction_vec).reshape(row_count, quarter_len)
         direct = jnp.einsum("jiq,jq->i", tiles, column_vec, precision=lax.Precision.HIGHEST)
         extra = obs_error * direction_vec
         own_part = lax.psum_scatter(direct, ("col", "sub"), scatter_dimension=0, tiled=True)

time: 208 us -> 218 us (1.048)
  starting transfers between devices: 6.32 us -> 27.5 us
  blocking collectives: 123 us -> 104 us
  waiting for transfers between devices: 29.8 us -> 34.6 us
  local copies, waits for them, and re-layouts: 8.07 us -> 11.1 us
    ppermute x0 -> x14, starting transfers between devices: none -> 21.2 us  [the longest x6 21.1 us: track_seats_all(): piece_next = jax.lax.ppermute(piece_next, comm_axis, inbox)]
    all_gather x2 -> x0, blocking collectives: 18.2 us -> none  [per_device(): lax.all_gather(direction_vec, ('row', 'sub'), axis=0, tiled=True)]
    ppermute x0 -> x14, waiting for transfers between devices: none -> 12.2 us  [the longest x8 12.1 us: track_seats_all(): tile_out = jax.lax.ppermute(tile_out, comm_axis, buffer)]
    all_gather x1, waiting for transfers between devices: 15.3 us -> 7.88 us  [per_device(): piece = lax.all_gather(own_quarter[None], 'row', axis=0, tiled=True)]
    dynamic_update_slice x0 -> x15, local copies, waits for them, and re-layouts: none -> 3 us  [the longest x8 1.57 us: track_seats_all(): lax.dynamic_update_slice_in_dim(m_next, tile_out, (value_now - dev_i) % r...]
  transfers between devices with their start and end apart: 2 -> 16, of which waited for: 2 -> 12; matrix products, arithmetic and copies ran while one was open for 1% -> 2% of each run, Pallas kernels for 0% -> 0%
where the time goes in v1:
time: 218 us; the launch traced here: 217 us
  blocking collectives  104 us (48%)
  waiting for transfers between devices  34.6 us (16%)
  starting transfers between devices  27.5 us (13%)
  between operations  18.8 us (9%)
  local copies, waits for them, and re-layouts  11.1 us (5%)
  matrix products  10.1 us (5%)
  loops' own time  7.89 us (4%)
  other arithmetic  3.44 us (2%)
    psum x2, blocking collectives, squares(): return lax.psum(jnp.sum(residual * residual), ('row', 'col', 'sub'))  61.7 us
    psum x1, blocking collectives, per_device(): lax.psum(jnp.sum(direction_vec * image), ('row', 'col', 'sub'))  30.1 us
    ppermute x6, starting transfers between devices, track_seats_all(): piece_next = jax.lax.ppermute(piece_next, comm_axis, inbox)  21.1 us
    all_to_all x1, waiting for transfers between devices, per_device(): lax.all_to_all(anomalies, 'row', split_axis=1, concat_axis=0, tiled=True)  14.5 us
    unnamed x2, blocking collectives  12.2 us
    ppermute x8, waiting for transfers between devices, track_seats_all(): tile_out = jax.lax.ppermute(tile_out, comm_axis, buffer)  12.1 us
    another operation x1, loops' own time, per_device(): tiles = lax.map(one_entry, (piece, indices))  7.89 us
    all_gather x1, waiting for transfers between devices, per_device(): piece = lax.all_gather(own_quarter[None], 'row', axis=0, tiled=True)  7.88 us
  transfers between devices with their start and end apart: 16, of which 12 were waited for; matrix products, arithmetic and copies ran while one was open for 2% of the time, Pallas kernels for 0%

profile of v1, /device:TPU:0, one launch (start us, length us, event | category | flops | bytes accessed | tf_op | source)
XLA Modules:
  0.0 217.5 jit_solution(3285375980401743923)
XLA Ops:
  7.2 1.9 copy.16
  9.1 6.3 %all-to-all-start = ((bf16[128,4,512]{2,0,1:T(8,128)(2,1)}), bf16[128,4,512]{2,0,1:T(8,128)(2,1)S(1)}, u32[]{:S(2)}, u32[]{:S(2)}) async-start(bf16[128,4,512]{2,0,1:T(8,128)(2,1)} %bitcast.39), calls=%async_computation | async-start | bytes 1048576 | tf_op jit(solution)/shard_map/all_to_all | solution.py:61
  15.4 14.5 %all-to-all-done = bf16[128,4,512]{2,0,1:T(8,128)(2,1)S(1)} async-done(((bf16[128,4,512]{2,0,1:T(8,128)(2,1)}), bf16[128,4,512]{2,0,1:T(8,128)(2,1)S(1)}, u32[]{:S(2)}, u32[]{:S(2)}) %all-to-all-start) | async-done | bytes 524320 | tf_op jit(solution)/shard_map/all_to_all | solution.py:61
  29.9 0.7 constant_dynamic-slice_fusion.3
  30.7 3.5 %collective-permute-start.1 = (f32[128]{0:T(128)S(1)}, f32[128]{0:T(128)S(1)}, u32[]{:S(2)}, u32[]{:S(2)}) collective-permute-start(f32[128]{0:T(128)S(1)} %copy-done.2), channel_id=1, source_target_pairs={{0,13},{1,0},{4,1},{5,4},{8,5},{9,8},{12,9},{13,12},{2,15},{3,2},{... | collective-permute-start | bytes 1544 | tf_op jit(solution)/shard_map/ppermute | solution.py:29
  34.3 0.7 maximum_bitcast_fusion
  35.0 0.1 dynamic_slice.32
  35.1 0.4 collective-permute-done
  35.5 0.2 dynamic_update_slice.52
  35.7 3.6 %collective-permute-start.3 = (f32[128]{0:T(128)S(1)}, f32[128]{0:T(128)S(1)}, u32[]{:S(2)}, u32[]{:S(2)}) collective-permute-start(f32[128]{0:T(128)S(1)} %collective-permute-done.1), channel_id=1, source_target_pairs={{0,13},{1,0},{4,1},{5,4},{8,5},{9,8},{12,9},{13,12},{2,15},{3,2},{... | collective-permute-start | bytes 1544 | tf_op jit(solution)/shard_map/ppermute | solution.py:29
  39.2 1.0 collective-permute-done.2
  40.3 0.6 dynamic-slice
  40.8 3.5 %collective-permute-start.5 = (f32[128]{0:T(128)S(1)}, f32[128]{0:T(128)S(1)}, u32[]{:S(2)}, u32[]{:S(2)}) collective-permute-start(f32[128]{0:T(128)S(1)} %collective-permute-done.3), channel_id=1, source_target_pairs={{0,13},{1,0},{4,1},{5,4},{8,5},{9,8},{12,9},{13,12},{2,15},{3,2},{... | collective-permute-start | bytes 1544 | tf_op jit(solution)/shard_map/ppermute | solution.py:29
  44.4 0.6 collective-permute-done.4
  45.7 0.2 dynamic_update_slice.53
  45.9 0.2 dynamic_update_slice.54
  46.1 0.2 dynamic_update_slice.55
  46.3 0.2 dynamic_update_slice.56
  46.5 0.2 dynamic_update_slice.57
  46.7 0.2 dynamic_update_slice.58
  46.9 2.8 %collective-permute-done.6 = f32[128]{0:T(128)S(1)} collective-permute-done((f32[128]{0:T(128)S(1)}, f32[128]{0:T(128)S(1)}, u32[]{:S(2)}, u32[]{:S(2)}) %collective-permute-start.6) | collective-permute-done | bytes 544 | tf_op jit(solution)/shard_map/ppermute | solution.py:24
  49.8 0.2 dynamic_update_slice.59
  50.0 7.9 %all-gather.3.cloned.1.call-done = bf16[2048,256]{1,0:T(8,128)(2,1)} async-done(((bf16[512,256]{1,0:T(8,128)(2,1)}), bf16[2048,256]{1,0:T(8,128)(2,1)}) %all-gather.3.cloned.1.call-update) | async-done | bytes 1048592 | tf_op jit(solution)/shard_map/all_gather | solution.py:75
  57.9 20.4 %while.10 = (s32[]{:T(128)}, f32[4,512,256]{1,2,0:T(8,128)S(1)}, bf16[4,512,256]{2,1,0:T(8,128)(2,1)}, bf16[512,512]{1,0:T(8,128)(2,1)S(1)}, s32[4]{0:T(128)S(1)...) while((s32[]{:T(128)}, f32[4,512,256]{1,2,0:T(8,128)S(1)}, ...), condition=%wide.region_3.4_spmd, body=%wide.region_2.3_spmd.sunk | while | flops 135135232 | bytes 1317555 | solution.py:77
  57.9 0.6 dynamic_slice.56
  60.4 0.6 dynamic_slice.57
  61.0 1.9 fusion.22
  62.9 0.6 dynamic_slice.56
  65.5 0.6 dynamic_slice.57
  66.1 1.9 fusion.22
  68.0 0.6 dynamic_slice.56
  70.6 0.6 dynamic_slice.57
  71.2 1.9 fusion.22
  73.1 0.6 dynamic_slice.56
  75.7 0.6 dynamic_slice.57
  76.3 1.9 fusion.22
  78.2 1.2 fusion.10
  79.4 6.4 %all-reduce = f32[512]{0:T(512)S(1)} all-reduce(f32[512]{0:T(512)S(1)} %bitcast.63), channel_id=3, replica_groups=mesh['group'=2,'row'=4,'col'=2,'sub'=2] {'col','sub'}, use_global_device_ids=true, to_apply=%region_4.5.clone | all-reduce | flops 512 | bytes 4096
  85.9 0.7 multiply_reduce_fusion.2
  86.5 31.6 %all-reduce.2 = (f32[]{:T(128)}, f32[]{:T(128)}) all-reduce(f32[]{:T(128)} %get-tuple-element.46, f32[]{:T(128)} %get-tuple-element.45), channel_id=1, replica_groups=mesh['group'=2,'row'=4,'col'=2,'sub'=2] {'row','col','sub'}, use_global_device_ids=true, to_apply=%region_1.2 | all-reduce | flops 2 | bytes 16 | tf_op jit(solution)/shard_map/psum | solution.py:40
  119.5 0.7 multiply_reduce_fusion.1
  120.2 30.1 %psum.30 = f32[]{:T(128)} all-reduce(f32[]{:T(128)} %get-tuple-element.67), channel_id=1, replica_groups=mesh['group'=2,'row'=4,'col'=2,'sub'=2] {'row','col','sub'}, use_global_device_ids=true, to_apply=%region_8.9 | all-reduce | flops 1 | bytes 8 | tf_op jit(solution)/shard_map/psum | solution.py:40
  151.6 0.1 fusion.9
  151.8 3.5 %collective-permute-start.8 = (f32[128]{0:T(128)S(1)}, f32[128]{0:T(128)S(1)}, u32[]{:S(2)}, u32[]{:S(2)}) collective-permute-start(f32[128]{0:T(128)S(1)} %get-tuple-element.66), channel_id=1, source_target_pairs={{0,13},{1,0},{4,1},{5,4},{8,5},{9,8},{12,9},{13,12},{2,15},{3,2},{... | collective-permute-start | bytes 1544 | tf_op jit(solution)/shard_map/ppermute | solution.py:29
  155.3 1.2 collective-permute-done.7
  156.5 0.1 collective-permute-done.8
  156.6 3.5 %collective-permute-start.10 = (f32[128]{0:T(128)S(1)}, f32[128]{0:T(128)S(1)}, u32[]{:S(2)}, u32[]{:S(2)}) collective-permute-start(f32[128]{0:T(128)S(1)} %collective-permute-done.8), channel_id=1, source_target_pairs={{0,13},{1,0},{4,1},{5,4},{8,5},{9,8},{12,9},{13,12},{2,15},{3,2},{... | collective-permute-start | bytes 1544 | tf_op jit(solution)/shard_map/ppermute | solution.py:29
  160.1 1.2 collective-permute-done.9
  161.3 0.1 collective-permute-done.10
  161.4 3.5 %collective-permute-start.12 = (f32[128]{0:T(128)S(1)}, f32[128]{0:T(128)S(1)}, u32[]{:S(2)}, u32[]{:S(2)}) collective-permute-start(f32[128]{0:T(128)S(1)} %collective-permute-done.10), channel_id=1, source_target_pairs={{0,13},{1,0},{4,1},{5,4},{8,5},{9,8},{12,9},{13,12},{2,15},{3,2},{... | collective-permute-start | bytes 1544 | tf_op jit(solution)/shard_map/ppermute | solution.py:29
  164.8 1.2 collective-permute-done.11
  166.1 0.2 dynamic_update_slice.61
  166.2 0.2 dynamic_update_slice.62
  166.4 0.2 dynamic_update_slice.63
  166.6 0.2 dynamic_update_slice.64
  166.8 0.2 dynamic_update_slice.65
  167.0 0.2 dynamic_update_slice.66
  167.3 3.6 %collective-permute-done.13 = f32[128]{0:T(128)S(1)} collective-permute-done((f32[128]{0:T(128)S(1)}, f32[128]{0:T(128)S(1)}, u32[]{:S(2)}, u32[]{:S(2)}) %collective-permute-start.13) | collective-permute-done | bytes 544 | tf_op jit(solution)/shard_map/ppermute | solution.py:24
  170.8 0.2 dynamic_update_slice.67
  171.0 1.2 fusion.11
  172.2 5.7 %all-reduce.1 = f32[512]{0:T(512)S(1)} all-reduce(f32[512]{0:T(512)S(1)} %bitcast.62), channel_id=4, replica_groups=mesh['group'=2,'row'=4,'col'=2,'sub'=2] {'col','sub'}, use_global_device_ids=true, to_apply=%region_9.10.clone | all-reduce | flops 512 | bytes 4096
  177.9 0.7 multiply_reduce_fusion
  178.6 30.1 %psum.31 = f32[]{:T(128)} all-reduce(f32[]{:T(128)} %multiply_reduce_fusion), channel_id=1, replica_groups=mesh['group'=2,'row'=4,'col'=2,'sub'=2] {'row','col','sub'}, use_global_device_ids=true, to_apply=%region_11.12 | all-reduce | flops 1 | bytes 8 | tf_op jit(solution)/shard_map/psum | solution.py:88
  210.0 0.6 multiply_subtract_fusion
  (33 shorter events, 0.2 us)
Async XLA Ops:
  7.2 33.1 %copy-start.3 = (u32[32]{0:T(128)S(1)}, u32[32]{0:T(128)}, u32[]{:S(2)}) copy-start(u32[32]{0:T(128)} %constant.132) | copy-start | bytes 388
  7.2 23.5 %copy-start.2 = (f32[128]{0:T(128)S(1)}, f32[128]{0:T(128)}, u32[]{:S(2)}) copy-start(f32[128]{0:T(128)} %param.8) | copy-start | bytes 1540
  7.2 27.1 %copy-start = (f32[2048]{0:T(1024)S(1)}, f32[2048]{0:T(1024)}, u32[]{:S(2)}) copy-start(f32[2048]{0:T(1024)} %param.10) | copy-start | bytes 24580
  9.1 20.8 %all-to-all-start = ((bf16[128,4,512]{2,0,1:T(8,128)(2,1)}), bf16[128,4,512]{2,0,1:T(8,128)(2,1)S(1)}, u32[]{:S(2)}, u32[]{:S(2)}) async-start(bf16[128,4,512]{2,0,1:T(8,128)(2,1)} %bitcast.39), calls=%async_computation | async-start | bytes 1048576 | tf_op jit(solution)/shard_map/all_to_all | solution.py:61
  15.4 42.4 %all-gather.3.cloned.1.call-start = ((), (), s32[]{:S(2)}) async-start(), calls=%async_computation.1 | async-start | bytes 1310720 | tf_op jit(solution)/shard_map/all_gather | solution.py:75
  30.7 4.8 %collective-permute-start = (f32[128]{0:T(128)S(1)}, f32[128]{0:T(128)S(1)}, u32[]{:S(2)}, u32[]{:S(2)}) collective-permute-start(f32[128]{0:T(128)S(1)} %copy-done.2), channel_id=1, source_target_pairs={{0,1},{1,4},{4,5},{5,8},{8,9},{9,12},{12,13},{13,0},{2,3},{3,6},{6... | collective-permute-start | bytes 1544 | tf_op jit(solution)/shard_map/ppermute | solution.py:24
  30.7 5.0 %collective-permute-start.1 = (f32[128]{0:T(128)S(1)}, f32[128]{0:T(128)S(1)}, u32[]{:S(2)}, u32[]{:S(2)}) collective-permute-start(f32[128]{0:T(128)S(1)} %copy-done.2), channel_id=1, source_target_pairs={{0,13},{1,0},{4,1},{5,4},{8,5},{9,8},{12,9},{13,12},{2,15},{3,2},{... | collective-permute-start | bytes 1544 | tf_op jit(solution)/shard_map/ppermute | solution.py:29
  35.5 4.8 %collective-permute-start.2 = (f32[128]{0:T(128)S(1)}, f32[128]{0:T(128)S(1)}, u32[]{:S(2)}, u32[]{:S(2)}) collective-permute-start(f32[128]{0:T(128)S(1)} %collective-permute-done), channel_id=1, source_target_pairs={{0,1},{1,4},{4,5},{5,8},{8,9},{9,12},{12,13},{13,0},{2,3},{3,6},{6... | collective-permute-start | bytes 1544 | tf_op jit(solution)/shard_map/ppermute | solution.py:24
  35.7 5.2 %collective-permute-start.3 = (f32[128]{0:T(128)S(1)}, f32[128]{0:T(128)S(1)}, u32[]{:S(2)}, u32[]{:S(2)}) collective-permute-start(f32[128]{0:T(128)S(1)} %collective-permute-done.1), channel_id=1, source_target_pairs={{0,13},{1,0},{4,1},{5,4},{8,5},{9,8},{12,9},{13,12},{2,15},{3,2},{... | collective-permute-start | bytes 1544 | tf_op jit(solution)/shard_map/ppermute | solution.py:29
  40.2 4.8 %collective-permute-start.4 = (f32[128]{0:T(128)S(1)}, f32[128]{0:T(128)S(1)}, u32[]{:S(2)}, u32[]{:S(2)}) collective-permute-start(f32[128]{0:T(128)S(1)} %collective-permute-done.2), channel_id=1, source_target_pairs={{0,1},{1,4},{4,5},{5,8},{8,9},{9,12},{12,13},{13,0},{2,3},{3,6},{6... | collective-permute-start | bytes 1544 | tf_op jit(solution)/shard_map/ppermute | solution.py:24
  40.8 5.9 %collective-permute-start.5 = (f32[128]{0:T(128)S(1)}, f32[128]{0:T(128)S(1)}, u32[]{:S(2)}, u32[]{:S(2)}) collective-permute-start(f32[128]{0:T(128)S(1)} %collective-permute-done.3), channel_id=1, source_target_pairs={{0,13},{1,0},{4,1},{5,4},{8,5},{9,8},{12,9},{13,12},{2,15},{3,2},{... | collective-permute-start | bytes 1544 | tf_op jit(solution)/shard_map/ppermute | solution.py:29
  45.0 4.8 %collective-permute-start.6 = (f32[128]{0:T(128)S(1)}, f32[128]{0:T(128)S(1)}, u32[]{:S(2)}, u32[]{:S(2)}) collective-permute-start(f32[128]{0:T(128)S(1)} %collective-permute-done.4), channel_id=1, source_target_pairs={{0,1},{1,4},{4,5},{5,8},{8,9},{9,12},{12,13},{13,0},{2,3},{3,6},{6... | collective-permute-start | bytes 1544 | tf_op jit(solution)/shard_map/ppermute | solution.py:24
  78.2 7.6 %copy-start.1 = (f32[128]{0:T(128)S(1)}, f32[128]{0:T(128)}, u32[]{:S(2)}) copy-start(f32[128]{0:T(128)} %param.9) | copy-start | bytes 1540
  151.7 4.8 %collective-permute-start.7 = (f32[128]{0:T(128)S(1)}, f32[128]{0:T(128)S(1)}, u32[]{:S(2)}, u32[]{:S(2)}) collective-permute-start(f32[128]{0:T(128)S(1)} %get-tuple-element.66), channel_id=1, source_target_pairs={{0,1},{1,4},{4,5},{5,8},{8,9},{9,12},{12,13},{13,0},{2,3},{3,6},{6... | collective-permute-start | bytes 1544 | tf_op jit(solution)/shard_map/ppermute | solution.py:24
  151.8 4.8 %collective-permute-start.8 = (f32[128]{0:T(128)S(1)}, f32[128]{0:T(128)S(1)}, u32[]{:S(2)}, u32[]{:S(2)}) collective-permute-start(f32[128]{0:T(128)S(1)} %get-tuple-element.66), channel_id=1, source_target_pairs={{0,13},{1,0},{4,1},{5,4},{8,5},{9,8},{12,9},{13,12},{2,15},{3,2},{... | collective-permute-start | bytes 1544 | tf_op jit(solution)/shard_map/ppermute | solution.py:29
  156.5 4.8 %collective-permute-start.9 = (f32[128]{0:T(128)S(1)}, f32[128]{0:T(128)S(1)}, u32[]{:S(2)}, u32[]{:S(2)}) collective-permute-start(f32[128]{0:T(128)S(1)} %collective-permute-done.7), channel_id=1, source_target_pairs={{0,1},{1,4},{4,5},{5,8},{8,9},{9,12},{12,13},{13,0},{2,3},{3,6},{6... | collective-permute-start | bytes 1544 | tf_op jit(solution)/shard_map/ppermute | solution.py:24
  156.6 4.8 %collective-permute-start.10 = (f32[128]{0:T(128)S(1)}, f32[128]{0:T(128)S(1)}, u32[]{:S(2)}, u32[]{:S(2)}) collective-permute-start(f32[128]{0:T(128)S(1)} %collective-permute-done.8), channel_id=1, source_target_pairs={{0,13},{1,0},{4,1},{5,4},{8,5},{9,8},{12,9},{13,12},{2,15},{3,2},{... | collective-permute-start | bytes 1544 | tf_op jit(solution)/shard_map/ppermute | solution.py:29
  161.3 4.8 %collective-permute-start.11 = (f32[128]{0:T(128)S(1)}, f32[128]{0:T(128)S(1)}, u32[]{:S(2)}, u32[]{:S(2)}) collective-permute-start(f32[128]{0:T(128)S(1)} %collective-permute-done.9), channel_id=1, source_target_pairs={{0,1},{1,4},{4,5},{5,8},{8,9},{9,12},{12,13},{13,0},{2,3},{3,6},{6... | collective-permute-start | bytes 1544 | tf_op jit(solution)/shard_map/ppermute | solution.py:24
  161.4 5.7 %collective-permute-start.12 = (f32[128]{0:T(128)S(1)}, f32[128]{0:T(128)S(1)}, u32[]{:S(2)}, u32[]{:S(2)}) collective-permute-start(f32[128]{0:T(128)S(1)} %collective-permute-done.10), channel_id=1, source_target_pairs={{0,13},{1,0},{4,1},{5,4},{8,5},{9,8},{12,9},{13,12},{2,15},{3,2},{... | collective-permute-start | bytes 1544 | tf_op jit(solution)/shard_map/ppermute | solution.py:29
  166.1 4.8 %collective-permute-start.13 = (f32[128]{0:T(128)S(1)}, f32[128]{0:T(128)S(1)}, u32[]{:S(2)}, u32[]{:S(2)}) collective-permute-start(f32[128]{0:T(128)S(1)} %collective-permute-done.11), channel_id=1, source_target_pairs={{0,1},{1,4},{4,5},{5,8},{8,9},{9,12},{12,13},{13,0},{2,3},{3,6},{6... | collective-permute-start | bytes 1544 | tf_op jit(solution)/shard_map/ppermute | solution.py:24
Sparse Core Ops, SparseCore 0:
  30.8 27.0 all-gather.2
